TPU v7x, 32 devices: a whole 2x2x4 slice. The times are simulated.
32 devices in a mesh: dp: 4 (over z), vocab: 8 (over y, x, core).
Axes of the slice: x: 2, y: 2, z: 4, core: 2. Of those that a mesh axis runs over, the one named last changes fastest.
Arguments:
- query_hidden: bfloat16 [128, 4096], P('dp', 'vocab'), may hold values from -6 to 6
- passage_hidden_rows: bfloat16 [384, 4096], P('dp', 'vocab'), may hold values from -6 to 6
- head_weight: bfloat16 [4096, 128256], P(None, ('dp', 'vocab')), may hold values from -0.09375 to 0.09375
- head_bias: bfloat16 [128256], P(('dp', 'vocab')), may hold values from -4 to 4
- query_mask: int32 [8, 16], P('dp'), may hold values from 0 to 1, as said below
- passage_mask: int32 [8, 48], P('dp'), may hold values from 0 to 1, as said below
- positives: int32 [8], P('dp'), may hold values from 0 to 7, as said below
Outputs:
- loss: float32 [], replicated
- query_grad: bfloat16 [128, 4096], P('dp', 'vocab')
- passage_grad: bfloat16 [384, 4096], P('dp', 'vocab')
Inputs may be any that keep to these rules, and one draw needn't show every extreme that they name: `query_mask`: each row holds 4 or more ones from its first token on, then zeros. `passage_mask`: each row holds 12 or more ones from its first token on, then zeros. `positives`: query i's positive is a passage of its own group: it lies in [(i // 2) * 2, (i // 2 + 1) * 2).
All inputs are finite; a program needn't handle non-finite values.
Results may differ from a plain program's by a relative error of at most 0.013.
Values may be sent and summed in bfloat16 or wider, within the bound.
A program may use at most 128 MiB of HBM per device.

v0:
```python
import jax
import jax.numpy as jnp
from jax import lax
from jax.sharding import PartitionSpec as P

logit_divisor = 50.0
loss_scale = 1048576.0
epsilon = 1e-06


def pool_tokens(raw_scores_matrix, token_mask):
    text_series, span_extent = token_mask.shape
    lexical_response = jnp.log1p(jax.nn.softplus(raw_scores_matrix)).reshape(
        text_series, span_extent, -1
    )
    retained_flag = token_mask.astype(jnp.float32)
    term_importance = retained_flag[:, :, None] * jnp.exp(lexical_response)
    weight_sum = jnp.sum(term_importance, axis=1)
    term_total_count = jnp.sum(retained_flag, axis=1)[:, None]
    return (jnp.log(weight_sum / term_total_count), term_importance, weight_sum)


def spread(rep_grad, term_importance, weight_sum, raw_scores_matrix):
    text_series, span_extent, columns = term_importance.shape
    token_share = term_importance / weight_sum[:, None, :] * rep_grad[:, None, :]
    act_slope = jax.nn.sigmoid(raw_scores_matrix) / (1.0 + jax.nn.softplus(raw_scores_matrix))
    return token_share.reshape(text_series * span_extent, columns) * act_slope


def contrast(dots, query_sq, passage_sq, targets):
    question_length_measure = jnp.sqrt(query_sq + epsilon)
    document_length_measure = jnp.sqrt(passage_sq + epsilon)
    multiplier_coefficient = logit_divisor / (
        question_length_measure[:, None] * document_length_measure[None, :]
    )
    scores = dots * multiplier_coefficient
    exp_scores = jnp.exp(scores)
    exp_total = jnp.sum(exp_scores, axis=1)
    onehot = (targets[:, None] == jnp.arange(dots.shape[1], dtype=jnp.int32)[None, :]).astype(
        jnp.float32
    )
    loss = jnp.mean(jnp.log(exp_total) - jnp.sum(onehot * scores, axis=1))
    score_grad = (exp_scores / exp_total[:, None] - onehot) * (loss_scale / dots.shape[0])
    dots_grad = score_grad * multiplier_coefficient
    score_back = score_grad * scores
    query_coef = -jnp.sum(score_back, axis=1) / (query_sq + epsilon)
    passage_coef = -jnp.sum(score_back, axis=0) / (passage_sq + epsilon)
    return (loss, dots_grad, query_coef, passage_coef)


def shards(
    query_hidden, passage_hidden_rows, head_weight, head_bias, query_mask, passage_mask, positives
):
    groups = lax.axis_size("dp")
    bias_row = head_bias.astype(jnp.float32)
    vocab_cols = head_weight.shape[1]
    query_cols, passage_cols = (
        lax.all_gather(query_hidden, "vocab", axis=1, tiled=True),
        lax.all_gather(passage_hidden_rows, "vocab", axis=1, tiled=True),
    )
    question_lines, passage_rows, search_flags, passage_marks, targets = (
        lax.all_gather(query_cols, "dp", axis=0, tiled=True),
        lax.all_gather(passage_cols, "dp", axis=0, tiled=True),
        lax.all_gather(query_mask, "dp", axis=0, tiled=True),
        lax.all_gather(passage_mask, "dp", axis=0, tiled=True),
        lax.all_gather(positives, "dp", axis=0, tiled=True),
    )
    query_logits = (
        jnp.dot(question_lines, head_weight, preferred_element_type=jnp.float32) + bias_row
    )
    passage_logits = (
        jnp.dot(passage_rows, head_weight, preferred_element_type=jnp.float32) + bias_row
    )
    query_rep, query_weight, query_total = pool_tokens(query_logits, search_flags)
    passage_rep, passage_weight, passage_total = pool_tokens(passage_logits, passage_marks)
    local_dots = jnp.einsum("qv,pv->qp", query_rep, passage_rep, precision=lax.Precision.HIGHEST)
    dots, query_sq, passage_sq = lax.psum(
        (
            local_dots,
            jnp.sum(query_rep * query_rep, axis=1),
            jnp.sum(passage_rep * passage_rep, axis=1),
        ),
        ("dp", "vocab"),
    )
    loss, dots_grad, query_coef, passage_coef = contrast(dots, query_sq, passage_sq, targets)
    query_rep_grad = (
        jnp.einsum("qp,pv->qv", dots_grad, passage_rep, precision=lax.Precision.HIGHEST)
        + query_coef[:, None] * query_rep
    )
    passage_rep_grad = (
        jnp.einsum("qp,qv->pv", dots_grad, query_rep, precision=lax.Precision.HIGHEST)
        + passage_coef[:, None] * passage_rep
    )
    query_dlog = spread(query_rep_grad, query_weight, query_total, query_logits).astype(
        jnp.bfloat16
    )
    passage_dlog = spread(passage_rep_grad, passage_weight, passage_total, passage_logits).astype(
        jnp.bfloat16
    )
    query_group = query_dlog.reshape(groups, -1, vocab_cols)
    passage_group = passage_dlog.reshape(groups, -1, vocab_cols)
    query_count = query_group.shape[1]
    combined = jnp.concatenate((query_group, passage_group), 1).reshape(-1, vocab_cols)
    contract = (((1,), (1,)), ((), ()))
    summed = lax.psum_scatter(
        lax.dot_general(head_weight, combined, contract, preferred_element_type=jnp.float32).astype(
            jnp.bfloat16
        ),
        "vocab",
        scatter_dimension=0,
        tiled=True,
    )
    grad_rows = (
        lax.psum_scatter(summed, "dp", scatter_dimension=1, tiled=True).astype(jnp.float32).T
    )
    query_grad = grad_rows[:query_count].astype(jnp.bfloat16)
    passage_grad = grad_rows[query_count:].astype(jnp.bfloat16)
    return (loss, query_grad, passage_grad)


def solution(mesh):
    placed = (
        P("dp", "vocab"),
        P("dp", "vocab"),
        P(None, ("dp", "vocab")),
        P(("dp", "vocab")),
        P("dp", None),
        P("dp", None),
        P("dp"),
    )
    return jax.shard_map(
        shards,
        mesh=mesh,
        in_specs=placed,
        out_specs=(P(), P("dp", "vocab"), P("dp", "vocab")),
        check_vma=False,
    )
```

profile of v0, /device:TPU:0, one launch (start us, length us, event | category | flops | bytes accessed | tf_op | source)
XLA Modules:
  0.0 348.5 jit_solution(3847348254917007320)
XLA Ops:
  7.2 12.6 %all_gather.22 = bf16[32,4096]{1,0:T(8,128)(2,1)} all-gather(bf16[32,512]{1,0:T(8,128)(2,1)} %param.7), channel_id=1, replica_groups=mesh['dp'=4,'vocab'=8] {'vocab'}, dimensions={1}, use_global_device_ids=true | all-gather | bytes 294912 | tf_op jit(solution)/shard_map/all_gather | solution.py:58
  19.9 11.7 %all_gather.25 = bf16[96,4096]{1,0:T(8,128)(2,1)} all-gather(bf16[96,512]{1,0:T(8,128)(2,1)} %param.8), channel_id=1, replica_groups=mesh['dp'=4,'vocab'=8] {'vocab'}, dimensions={1}, use_global_device_ids=true | all-gather | bytes 884736 | tf_op jit(solution)/shard_map/all_gather | solution.py:59
  34.5 9.1 %all-reduce = s32[8]{0:T(128)S(1)} all-reduce(s32[8]{0:T(128)S(1)} %dynamic-update-slice), channel_id=1, replica_groups=mesh['dp'=4,'vocab'=8] {'dp'}, use_global_device_ids=true, to_apply=%add | all-reduce | flops 8 | bytes 64
  43.5 9.4 %all-gather = s32[4,2,16]{2,1,0:T(2,128)S(1)} all-gather(s32[1,2,16]{2,1,0:T(2,128)} %bitcast.36), channel_id=1, replica_groups=mesh['dp'=4,'vocab'=8] {'dp'}, dimensions={0}, use_global_device_ids=true | all-gather | bytes 640 | tf_op jit(solution)/shard_map/all_gather | solution.py:64
  53.2 8.5 %all-gather.1 = s32[4,2,48]{2,1,0:T(2,128)S(1)} all-gather(s32[1,2,48]{2,1,0:T(2,128)} %bitcast.37), channel_id=1, replica_groups=mesh['dp'=4,'vocab'=8] {'dp'}, dimensions={0}, use_global_device_ids=true | all-gather | bytes 1920 | tf_op jit(solution)/shard_map/all_gather | solution.py:65
  62.7 16.6 %log-plus-one_exponential_fusion.1 = (f32[128,4008]{0,1:T(8,128)}, f32[128,4008]{0,1:T(8,128)}) fusion(f32[4008]{0:T(1024)S(1)} %convert_element_type.28, bf16[128,4096]{1,0:T(8,128)(2,1)} %all-gather.5.cloned.1.call-done, bf16[4096,4008]{0,1:T(8,128)(2,1)} %param.9), kind=kOutput, calls=%fused_computation.13 | convolution fusion | flops 4206283776 | bytes 38002336 | tf_op jit(solution)/shard_map/dot_general | solution.py:69
  79.3 1.9 copy.22
  81.8 1.8 copy.24
  83.9 29.0 %all-gather.7.cloned.1.call-done = bf16[384,4096]{1,0:T(8,128)(2,1)} async-done(((bf16[96,4096]{1,0:T(8,128)(2,1)}), bf16[384,4096]{1,0:T(8,128)(2,1)}) %all-gather.7.cloned.1.call-update) | async-done | bytes 3145744 | tf_op jit(solution)/shard_map/all_gather | solution.py:63
  112.9 28.3 %log-plus-one_exponential_fusion = (f32[384,4008]{0,1:T(8,128)}, f32[384,4008]{0,1:T(8,128)}) fusion(f32[4008]{0:T(1024)S(1)} %convert_element_type.28, bf16[384,4096]{1,0:T(8,128)(2,1)} %all-gather.7.cloned.1.call-done, bf16[4096,4008]{0,1:T(8,128)(2,1)} %param.9), kind=kOutput, calls=%fused_computation.3 | convolution fusion | flops 12618851328 | bytes 48307872 | tf_op jit(solution)/shard_map/dot_general | solution.py:72
  141.2 6.5 %copy.23 = f32[384,4008]{1,0:T(8,128)} copy(f32[384,4008]{0,1:T(8,128)} %get-tuple-element.12) | data formatting | bytes 12312576 | tf_op jit(solution)/shard_map/exp | solution.py:17
  147.8 3.7 %multiply_reduce_fusion = f32[8,4008]{1,0:T(8,128)S(1)} fusion(f32[8,48,4008]{2,1,0:T(8,128)} %bitcast.24, f32[8,48]{1,0:T(8,128)S(1)} %bitcast.35), kind=kLoop, calls=%fused_computation.1 | loop fusion | flops 3046080 | bytes 6286080 | tf_op jit(solution)/shard_map/reduce_sum | solution.py:18
  152.2 39.1 %all-reduce.1 = (f32[8,8]{1,0:T(8,128)S(1)}, f32[8]{0:T(128)S(1)}, f32[8]{0:T(128)S(1)}) all-reduce(f32[8,8]{1,0:T(8,128)S(1)} %fusion.8, f32[8]{0:T(128)S(1)} %multiply_reduce_fusion.2, f32[8]{0:T(128)S(1)} %multiply_reduce_fusion.3), channel_id=1, replica_groups=mesh['dp'=4,'vocab'=8] {'dp','vocab'}, use_global_device_ids=true, to_apply=%region_4.5 | all-reduce | flops 80 | bytes 640 | tf_op jit(solution)/shard_map/psum | solution.py:77
  192.7 1.9 copy.25
  194.6 5.3 %multiply_convert_fusion.1 = bf16[128,4008]{0,1:T(8,128)(2,1)S(1)} fusion(f32[128,4008]{0,1:T(8,128)} %get-tuple-element.11, f32[128,4008]{0,1:T(8,128)} %copy.25, f32[128,4008]{0,1:T(8,128)} %copy.24, f32[128]{0:T(128)S(1)} %mul.122), kind=kLoop, calls=%fused_computation.12 | loop fusion | flops 8208384 | bytes 7182848 | tf_op jit(solution)/shard_map/convert_element_type | solution.py:94
  201.8 3.4 div.83
  205.2 6.5 %copy.27 = f32[384,4008]{0,1:T(8,128)} copy(f32[384,4008]{1,0:T(8,128)} %bitcast.25) | data formatting | bytes 12312576 | tf_op jit(solution)/shard_map/div | solution.py:25
  211.7 3.4 mul.140
  215.1 6.5 %copy.28 = f32[384,4008]{0,1:T(8,128)} copy(f32[384,4008]{1,0:T(8,128)} %bitcast.26) | data formatting | bytes 12312576 | tf_op jit(solution)/shard_map/mul | solution.py:25
  221.6 13.3 %multiply_convert_fusion = bf16[384,4008]{0,1:T(8,128)(2,1)} fusion(f32[384,4008]{0,1:T(8,128)} %copy.28, f32[384,4008]{0,1:T(8,128)} %copy.27, f32[384,4008]{0,1:T(8,128)} %get-tuple-element.13, f32[384]{0:T(512)S(1)} %mul.135, f32[4008]{0:T(1024)S(1)} %convert_element_type.28), kind=kLoop, calls=%fused_computation.2 | loop fusion | flops 26164224 | bytes 21564576 | tf_op jit(solution)/shard_map/convert_element_type | solution.py:97
  234.9 3.2 copy.29
  239.7 23.2 %fusion = bf16[4096,512]{0,1:T(8,128)(2,1)} fusion(bf16[512,4008]{1,0:T(8,128)(2,1)S(1)} %bitcast.30, bf16[4096,4008]{0,1:T(8,128)(2,1)} %param.9), kind=kOutput, calls=%fused_computation.6 | convolution fusion | flops 16812867584 | bytes 41132032 | tf_op jit(solution)/shard_map/dot_general | solution.py:106
  263.0 51.0 %reduce-scatter.3.cloned.1.call-done = bf16[512,512]{0,1:T(8,128)(2,1)} async-done(((bf16[4096,512]{0,1:T(8,128)(2,1)}), bf16[512,512]{0,1:T(8,128)(2,1)}) %reduce-scatter.3.cloned.1.call-update) | async-done | bytes 524304 | tf_op jit(solution)/shard_map/reduce_scatter | solution.py:105
  315.2 22.7 %reduce-scatter.5.cloned.1.call-done = bf16[512,128]{0,1:T(8,128)(2,1)} async-done(((bf16[512,512]{0,1:T(8,128)(2,1)}), bf16[512,128]{0,1:T(8,128)(2,1)}) %reduce-scatter.5.cloned.1.call-update) | async-done | bytes 131088 | tf_op jit(solution)/shard_map/reduce_scatter | solution.py:114
  (39 shorter events, 13.5 us)
Async XLA Ops:
  7.2 55.5 %all-gather.5.cloned.1.call-start = ((), (), s32[]{:S(2)}) async-start(), calls=%async_computation.2 | async-start | bytes 1310720 | tf_op jit(solution)/shard_map/all_gather | solution.py:62
  19.8 93.1 %all-gather.7.cloned.1.call-start = ((), (), s32[]{:S(2)}) async-start(), calls=%async_computation.3 | async-start | bytes 3932160 | tf_op jit(solution)/shard_map/all_gather | solution.py:63
  31.6 282.3 %reduce-scatter.3.cloned.1.call-start = ((), (), s32[]{:S(2)}) async-start(), calls=%async_computation.4 | async-start | bytes 4718592 | tf_op jit(solution)/shard_map/reduce_scatter | solution.py:105
  262.9 75.0 %reduce-scatter.5.cloned.1.call-start = ((), (), s32[]{:S(2)}) async-start(), calls=%async_computation.5 | async-start | bytes 655360 | tf_op jit(solution)/shard_map/reduce_scatter | solution.py:114
Sparse Core Ops, SparseCore 0:
  19.9 28.4 all-gather.4
  50.0 62.8 all-gather.6
  263.0 50.8 reduce-scatter.2
  316.1 21.8 reduce-scatter.4
where the time goes:
time: 349 us; the launch traced here: 348 us
  waiting for transfers between devices  103 us (30%)
  blocking collectives  90.4 us (26%)
  matrix products  69.3 us (20%)
  local copies, waits for them, and re-layouts  42.7 us (12%)
  other arithmetic  26.9 us (8%)
  between operations  16.3 us (5%)
    reduce_scatter x1, waiting for transfers between devices, shards(): lax.psum_scatter(lax.dot_general(head_weight, combined, contract, preferr...  51 us
    psum x1, blocking collectives, shards(): lax.psum((local_dots, jnp.sum(query_rep * query_rep, axis=1), jnp.sum(pas...  39.1 us
    all_gather x1, waiting for transfers between devices, shards(): lax.all_gather(passage_cols, 'dp', axis=0, tiled=True)  29 us
    dot_general x1, matrix products, shards(): jnp.dot(passage_rows, head_weight, preferred_element_type=jnp.float32)  28.3 us
    dot_general x1, matrix products, shards(): lax.dot_general(head_weight, combined, contract, preferred_element_type=j...  23.2 us
    reduce_scatter x1, waiting for transfers between devices, shards(): lax.psum_scatter(summed, 'dp', scatter_dimension=1, tiled=True)  22.7 us
    dot_general x1, matrix products, shards(): jnp.dot(question_lines, head_weight, preferred_element_type=jnp.float32)  16.6 us
    convert_element_type x1, other arithmetic, shards(): spread(passage_rep_grad, passage_weight, passage_total, passage_logits)  13.3 us
  transfers between devices with their start and end apart: 4, of which 3 were waited for; matrix products, arithmetic and copies ran while one was open for 7% of the time, Pallas kernels for 0%

commit v1 on v0

v1 whole, which is shorter than its diff:
```python
import functools

import jax
import jax.numpy as jnp
from jax import lax
from jax.experimental import pallas as pl
from jax.experimental.pallas import tpu as pltpu
from jax.sharding import PartitionSpec as P

logit_divisor = 50.0
loss_scale = 1048576.0
epsilon = 1e-06
HIGH = lax.Precision.HIGHEST


def segments(groups, seq_q, len_q, seq_p, len_p):
    rows = seq_q * len_q + seq_p * len_p
    found = []
    for g in range(groups):
        for i in range(seq_q):
            found.append((g * seq_q + i, g * rows + i * len_q, len_q))
        for j in range(seq_p):
            found.append(
                (groups * seq_q + g * seq_p + j, g * rows + seq_q * len_q + j * len_p, len_p)
            )
    return found


def forward_kernel(
    segs, cols, x_ref, w_ref, bias_ref, mask_ref, count_ref, sig_ref, rep_ref, inv_ref, gram_ref,
    xs, sums
):
    step = pl.program_id(0)
    blocks, rows, width = x_ref.shape
    tile = w_ref.shape[1]

    @pl.when(step == 0)
    def _():
        for v in range(blocks):
            xs[:, v * width : (v + 1) * width] = x_ref[v]
        gram_ref[...] = jnp.zeros_like(gram_ref)

    valid = lax.broadcasted_iota(jnp.int32, (1, tile), 1) < cols - step * tile
    logits = jnp.dot(xs[...], w_ref[...], preferred_element_type=jnp.float32)
    logits = logits + bias_ref[...].astype(jnp.float32)
    small = jnp.exp(-jnp.abs(logits))
    grown = 1.0 + small
    soft = jnp.maximum(logits, 0.0) + jnp.log(grown)
    keep = mask_ref[...]
    weight = keep * (1.0 + soft)
    share = keep * (jnp.where(logits >= 0.0, 1.0, small) / grown)
    sig_ref[...] = jnp.where(valid, share, 0.0).astype(sig_ref.dtype)
    for row, first, size in segs:
        sums[row : row + 1, :] = jnp.sum(weight[first : first + size], axis=0, keepdims=True)
    total = jnp.where(valid, sums[...], 1.0)
    rep = jnp.where(valid, jnp.log(total / count_ref[...]), 0.0)
    rep_ref[...] = rep
    inv_ref[...] = 1.0 / total
    gram_ref[...] += lax.dot_general(
        rep, rep, (((1,), (1,)), ((), ())), precision=HIGH, preferred_element_type=jnp.float32
    )


def contrast(gram, targets, queries):
    passages = gram.shape[0] - queries
    dots = gram[:queries, queries:]
    qq, pp = gram[:queries, :queries], gram[queries:, queries:]

    def eye(n):
        return (
            lax.broadcasted_iota(jnp.int32, (n, n), 0) == lax.broadcasted_iota(jnp.int32, (n, n), 1)
        ).astype(jnp.float32)

    q_col = jnp.sum(qq * eye(queries), axis=1, keepdims=True)
    p_row = jnp.sum(pp * eye(passages), axis=0, keepdims=True)
    scaling = logit_divisor / (jnp.sqrt(q_col + epsilon) * jnp.sqrt(p_row + epsilon))
    scores = dots * scaling
    exp_scores = jnp.exp(scores)
    exp_total = jnp.sum(exp_scores, axis=1, keepdims=True)
    onehot = (targets == lax.broadcasted_iota(jnp.int32, (queries, passages), 1)).astype(
        jnp.float32
    )
    losses = jnp.log(exp_total) - jnp.sum(onehot * scores, axis=1, keepdims=True)
    loss = jnp.sum(losses, axis=0, keepdims=True) / queries
    score_grad = (exp_scores / exp_total - onehot) * (loss_scale / queries)
    dots_grad = score_grad * scaling
    back = score_grad * scores
    q_coef = -jnp.sum(back, axis=1, keepdims=True) / (q_col + epsilon)
    p_coef = -jnp.sum(back, axis=0, keepdims=True) / (p_row + epsilon)
    return loss, dots_grad, q_coef, eye(passages) * p_coef


def backward_kernel(
    segs, queries, chunk, gram_ref, target_ref, rep_ref, inv_ref, sig_ref, w_ref, out_ref, loss_ref,
    dlog, scaled
):
    step = pl.program_id(0)
    cols = w_ref.shape[1]

    @pl.when(step == 0)
    def _():
        loss, dots_grad, q_coef, p_diag = contrast(gram_ref[...], target_ref[...], queries)
        loss_ref[...] = loss

        @pl.loop(0, dlog.shape[1] // chunk)
        def _(c):
            at = pl.ds(pl.multiple_of(c * chunk, chunk), chunk)
            rep = rep_ref[:, at]
            rep_q, rep_p = rep[:queries], rep[queries:]
            dot = functools.partial(
                lax.dot_general, precision=HIGH, preferred_element_type=jnp.float32
            )
            grad_q = dot(dots_grad, rep_p, (((1,), (0,)), ((), ()))) + q_coef * rep_q
            grad_p = dot(dots_grad, rep_q, (((0,), (0,)), ((), ()))) + dot(
                p_diag, rep_p, (((1,), (0,)), ((), ()))
            )
            inv = inv_ref[:, at]
            scaled[:queries] = grad_q * inv[:queries]
            scaled[queries:] = grad_p * inv[queries:]
            for row, first, size in segs:
                dlog[first : first + size, at] = (
                    sig_ref[first : first + size, at].astype(jnp.float32) * scaled[row : row + 1]
                ).astype(dlog.dtype)

    out_ref[0] = lax.dot_general(
        dlog[:, :cols], w_ref[...], (((1,), (1,)), ((), ())), preferred_element_type=jnp.float32
    ).astype(out_ref.dtype)


def compute_forward(x, head_weight, head_bias, keep, count, segs):
    blocks, rows, width = x.shape
    depth, cols = head_weight.shape
    tile = min(512, -(-cols // 128) * 128)
    tiles = -(-cols // tile)
    padded = tiles * tile
    block = tile if tile <= cols else cols
    if block != tile:
        tile, padded = cols, cols
    whole = lambda shape: pl.BlockSpec(shape, lambda i: (0,) * len(shape))
    seqs = count.shape[0]
    return pl.pallas_call(
        functools.partial(forward_kernel, segs, cols),
        grid=(tiles,),
        out_shape=(
            jax.ShapeDtypeStruct((rows, padded), jnp.bfloat16),
            jax.ShapeDtypeStruct((seqs, padded), jnp.float32),
            jax.ShapeDtypeStruct((seqs, padded), jnp.float32),
            jax.ShapeDtypeStruct((seqs, seqs), jnp.float32),
        ),
        in_specs=[
            whole(x.shape),
            pl.BlockSpec((depth, tile), lambda i: (0, i)),
            pl.BlockSpec((1, tile), lambda i: (0, i)),
            whole(keep.shape),
            whole(count.shape),
        ],
        out_specs=(
            pl.BlockSpec((rows, tile), lambda i: (0, i)),
            pl.BlockSpec((seqs, tile), lambda i: (0, i)),
            pl.BlockSpec((seqs, tile), lambda i: (0, i)),
            whole((seqs, seqs)),
        ),
        scratch_shapes=[
            pltpu.VMEM((rows, depth), jnp.bfloat16),
            pltpu.VMEM((seqs, tile), jnp.float32),
        ],
        compiler_params=pltpu.CompilerParams(vmem_limit_bytes=56 << 20),
    )(x, head_weight, head_bias.reshape(1, -1), keep, count)


def compute_backward(gram, targets, rep, inv, sig, head_weight, segs, blocks):
    depth, cols = head_weight.shape
    rows, padded = sig.shape
    seqs, queries = rep.shape[0], targets.shape[0]
    width = depth // blocks
    chunk = min(512, padded)
    whole = lambda shape: pl.BlockSpec(shape, lambda i: (0,) * len(shape))
    return pl.pallas_call(
        functools.partial(backward_kernel, segs, queries, chunk),
        grid=(blocks,),
        out_shape=(
            jax.ShapeDtypeStruct((blocks, rows, width), jnp.bfloat16),
            jax.ShapeDtypeStruct((1, 1), jnp.float32),
        ),
        in_specs=[
            whole(gram.shape),
            whole(targets.shape),
            whole(rep.shape),
            whole(inv.shape),
            whole(sig.shape),
            pl.BlockSpec((width, cols), lambda i: (i, 0)),
        ],
        out_specs=(pl.BlockSpec((1, rows, width), lambda i: (i, 0, 0)), whole((1, 1))),
        scratch_shapes=[
            pltpu.VMEM((rows, padded), jnp.bfloat16),
            pltpu.VMEM((seqs, chunk), jnp.float32),
        ],
        compiler_params=pltpu.CompilerParams(vmem_limit_bytes=56 << 20),
    )(gram, targets, rep, inv, sig, head_weight)


MESH = pl.DeviceIdType.MESH


def greet(peers):
    barrier = pltpu.get_barrier_semaphore()
    for peer in peers:
        pl.semaphore_signal(barrier, inc=1, device_id=peer, device_id_type=MESH)
    pl.semaphore_wait(barrier, len(peers))


def send(src, dst, send_sem, recv_sem, peer):
    return pltpu.make_async_remote_copy(
        src_ref=src,
        dst_ref=dst,
        send_sem=send_sem,
        recv_sem=recv_sem,
        device_id=peer,
        device_id_type=MESH,
    )


def places(groups, blocks):
    g, v = lax.axis_index("dp"), lax.axis_index("vocab")
    partner = v + 1 - 2 * lax.rem(v, 2)
    along_dp = [(lax.rem(g + k, groups), v) for k in range(1, groups)]
    along_vocab = [(g, lax.rem(v + 2 * j, blocks)) for j in range(1, blocks // 2)]
    return g, v, partner, along_dp, along_vocab


def gather_kernel(
    groups, blocks, own_ref, small_ref, out_ref, smalls_ref, local_sem, recv, recv_small, send_dp,
    send_small, send_vocab, send_pair
):
    g, v, partner, along_dp, along_vocab = places(groups, blocks)
    greet(along_dp + along_vocab + [(g, partner)])
    half = blocks // 2
    kept = pltpu.make_async_copy(own_ref, out_ref.at[v, g], local_sem.at[0])
    kept_small = pltpu.make_async_copy(small_ref, smalls_ref.at[g], local_sem.at[1])
    kept.start()
    kept_small.start()
    sent = []

    def go(src, vs, gs, sem, peer):
        copy = send(src, out_ref.at[vs, gs], sem, recv.at[vs, gs], peer)
        copy.start()
        sent.append(copy)

    def arrived(vs, gs):
        send(
            own_ref, out_ref.at[vs, gs], send_pair.at[0, 0], recv.at[vs, gs], (g, partner)
        ).wait_recv()

    for k, peer in enumerate(along_dp):
        go(own_ref, v, g, send_dp.at[k], peer)
    for k, peer in enumerate(along_dp):
        copy = send(small_ref, smalls_ref.at[g], send_small.at[k], recv_small.at[g], peer)
        copy.start()
        sent.append(copy)
    for k in range(groups):
        gs = lax.rem(g - k + groups, groups)
        src = own_ref
        if k:
            arrived(v, gs)
            src = out_ref.at[v, gs]
        for j, peer in enumerate(along_vocab):
            go(src, v, gs, send_vocab.at[k, j], peer)
        go(src, v, gs, send_pair.at[k, 0], (g, partner))
    for k in range(groups):
        gs = lax.rem(g - k + groups, groups)
        for j in range(1, half):
            vs = lax.rem(v - 2 * j + blocks, blocks)
            arrived(vs, gs)
            go(out_ref.at[vs, gs], vs, gs, send_pair.at[k, j], (g, partner))
    for k in range(groups):
        gs = lax.rem(g - k + groups, groups)
        for j in range(half):
            arrived(lax.rem(partner - 2 * j + blocks, blocks), gs)
        if k:
            send(
                small_ref, smalls_ref.at[gs], send_small.at[0], recv_small.at[gs], (g, partner)
            ).wait_recv()
    for copy in sent:
        copy.wait_send()
    kept.wait()
    kept_small.wait()


def gather_all(own, small, groups, blocks):
    half, dma = blocks // 2, pltpu.SemaphoreType.DMA
    anywhere = pl.BlockSpec(memory_space=pl.ANY)
    return pl.pallas_call(
        functools.partial(gather_kernel, groups, blocks),
        out_shape=(
            jax.ShapeDtypeStruct((blocks, groups) + own.shape, own.dtype),
            jax.ShapeDtypeStruct((groups,) + small.shape, small.dtype),
        ),
        in_specs=[anywhere, anywhere],
        out_specs=(anywhere, anywhere),
        scratch_shapes=[
            dma((2,)),
            dma((blocks, groups)),
            dma((groups,)),
            dma((max(groups - 1, 1),)),
            dma((max(groups - 1, 1),)),
            dma((groups, max(half - 1, 1))),
            dma((groups, half)),
        ],
        compiler_params=pltpu.CompilerParams(collective_id=0, has_side_effects=True),
    )(own, small)


def total_kernel(groups, blocks, part_ref, out_ref, buf, local_sem, recv_v, send_v, recv_g, send_g):
    g, v = lax.axis_index("dp"), lax.axis_index("vocab")
    along_dp = [(lax.rem(g + k, groups), v) for k in range(1, groups)]
    along_vocab = [(g, lax.rem(v + j, blocks)) for j in range(1, blocks)]
    greet(along_dp + along_vocab)
    kept = pltpu.make_async_copy(part_ref, buf.at[g, v], local_sem.at[0])
    kept.start()
    sent = []
    for j, peer in enumerate(along_vocab):
        copy = send(part_ref, buf.at[g, v], send_v.at[j], recv_v.at[v], peer)
        copy.start()
        sent.append(copy)
    kept.wait()
    for j in range(1, blocks):
        vs = lax.rem(v - j + blocks, blocks)
        send(part_ref, buf.at[g, vs], send_v.at[0], recv_v.at[vs], (g, vs)).wait_recv()
    for k, peer in enumerate(along_dp):
        copy = send(buf.at[g], buf.at[g], send_g.at[k], recv_g.at[g], peer)
        copy.start()
        sent.append(copy)
    for k in range(1, groups):
        gs = lax.rem(g - k + groups, groups)
        send(buf.at[gs], buf.at[gs], send_g.at[0], recv_g.at[gs], (gs, v)).wait_recv()
    total = jnp.zeros(out_ref.shape, jnp.float32)
    for a in range(groups):
        for b in range(blocks):
            total = total + buf[a, b]
    out_ref[...] = total
    for copy in sent:
        copy.wait_send()


def total_all(part, groups, blocks):
    dma = pltpu.SemaphoreType.DMA
    inside = pl.BlockSpec(memory_space=pltpu.VMEM)
    return pl.pallas_call(
        functools.partial(total_kernel, groups, blocks),
        out_shape=jax.ShapeDtypeStruct(part.shape, part.dtype),
        in_specs=[inside],
        out_specs=inside,
        scratch_shapes=[
            pltpu.VMEM((groups, blocks) + part.shape, jnp.float32),
            dma((1,)),
            dma((blocks,)),
            dma((max(blocks - 1, 1),)),
            dma((groups,)),
            dma((max(groups - 1, 1),)),
        ],
        compiler_params=pltpu.CompilerParams(collective_id=1, has_side_effects=True),
    )(part)


def scatter_kernel(
    groups, blocks, rows_q, a_ref, q_ref, p_ref, pair, pooled, peers, turned, last, recv_pair,
    send_pair, recv_vocab, send_vocab, recv_dp, send_dp
):
    g, v, partner, along_dp, along_vocab = places(groups, blocks)
    greet(along_dp + along_vocab + [(g, partner)])
    half = blocks // 2
    rows = a_ref.shape[1] // groups
    sent = []

    def go(src, dst, send_sem, recv_sem, peer):
        copy = send(src, dst, send_sem, recv_sem, peer)
        copy.start()
        sent.append(copy)

    order = list(range(1, half)) + [0]
    for j in order:
        w = lax.rem(partner + 2 * j, blocks)
        go(a_ref.at[w], pair.at[w // 2], send_pair.at[j], recv_pair.at[w // 2], (g, partner))
    for j in order:
        w = lax.rem(v + 2 * j, blocks)
        at = w // 2
        send(
            a_ref.at[w], pair.at[at], send_pair.at[0], recv_pair.at[at], (g, partner)
        ).wait_recv()
        pooled[at] = (
            a_ref[w].astype(jnp.float32) + pair[at].astype(jnp.float32)
        ).astype(pooled.dtype)
        if j:
            go(
                pooled.at[at],
                peers.at[v // 2],
                send_vocab.at[j - 1],
                recv_vocab.at[v // 2],
                along_vocab[j - 1],
            )
    for j in range(1, half):
        at = lax.rem(v - 2 * j + blocks, blocks) // 2
        send(
            pooled.at[at], peers.at[at], send_vocab.at[0], recv_vocab.at[at], (g, partner)
        ).wait_recv()

    def summed(gs):
        part = pl.ds(pl.multiple_of(gs * rows, rows), rows)
        out = pooled[v // 2, part].astype(jnp.float32)
        for j in range(1, half):
            at = lax.rem(v - 2 * j + blocks, blocks) // 2
            out = out + peers[at, part].astype(jnp.float32)
        return out

    for k, peer in enumerate(along_dp):
        turned[k] = summed(peer[0]).astype(turned.dtype)
        go(turned.at[k], last.at[g], send_dp.at[k], recv_dp.at[g], peer)
    out = summed(g)
    for k in range(1, groups):
        gs = lax.rem(g - k + groups, groups)
        send(turned.at[0], last.at[gs], send_dp.at[0], recv_dp.at[gs], (gs, v)).wait_recv()
        out = out + last[gs].astype(jnp.float32)
    q_ref[...] = out[:rows_q].astype(q_ref.dtype)
    p_ref[...] = out[rows_q:].astype(p_ref.dtype)
    for copy in sent:
        copy.wait_send()


def scatter_all(parts, groups, rows_q):
    blocks, tokens, width = parts.shape
    half, rows, dma = blocks // 2, tokens // groups, pltpu.SemaphoreType.DMA
    inside = pl.BlockSpec(memory_space=pltpu.VMEM)
    block = pltpu.VMEM((half, tokens, width), parts.dtype)
    return pl.pallas_call(
        functools.partial(scatter_kernel, groups, blocks, rows_q),
        out_shape=(
            jax.ShapeDtypeStruct((rows_q, width), parts.dtype),
            jax.ShapeDtypeStruct((rows - rows_q, width), parts.dtype),
        ),
        in_specs=[inside],
        out_specs=(inside, inside),
        scratch_shapes=[
            block,
            block,
            block,
            pltpu.VMEM((max(groups - 1, 1), rows, width), parts.dtype),
            pltpu.VMEM((groups, rows, width), parts.dtype),
            dma((half,)),
            dma((half,)),
            dma((half,)),
            dma((max(half - 1, 1),)),
            dma((groups,)),
            dma((max(groups - 1, 1),)),
        ],
        compiler_params=pltpu.CompilerParams(
            collective_id=2, has_side_effects=True, vmem_limit_bytes=48 << 20
        ),
    )(parts)


def shards(
    query_hidden, passage_hidden_rows, head_weight, head_bias, query_mask, passage_mask, positives
):
    groups, blocks = lax.axis_size("dp"), lax.axis_size("vocab")
    seq_q, len_q = query_mask.shape
    seq_p, len_p = passage_mask.shape
    rows_q = seq_q * len_q
    rows, width = rows_q + seq_p * len_p, query_hidden.shape[1]
    segs = segments(groups, seq_q, len_q, seq_p, len_p)

    own = jnp.concatenate((query_hidden, passage_hidden_rows), 0)
    small = jnp.concatenate((query_mask.reshape(-1), passage_mask.reshape(-1), positives))
    lanes = 128
    held = -(-small.shape[0] // (8 * lanes)) * 8 * lanes
    ints = small.shape[0]
    small = jnp.pad(small, (0, held - ints)).reshape(-1, lanes)
    x, small = gather_all(own, small, groups, blocks)
    x = x.reshape(blocks, groups * rows, width)
    small = small.reshape(groups, held)[:, :ints]
    targets = small[:, rows:].reshape(-1, 1)
    keep = small[:, :rows].astype(jnp.float32)
    count = jnp.concatenate(
        (
            jnp.sum(keep[:, :rows_q].reshape(-1, len_q), axis=1),
            jnp.sum(keep[:, rows_q:].reshape(-1, len_p), axis=1),
        )
    )[:, None]
    sig, rep, inv, gram = compute_forward(
        x, head_weight, head_bias, keep.reshape(-1, 1), count, segs
    )
    gram = total_all(gram, groups, blocks)
    grads, loss = compute_backward(gram, targets, rep, inv, sig, head_weight, segs, blocks)
    query_grad, passage_grad = scatter_all(grads, groups, rows_q)
    return (loss[0, 0], query_grad, passage_grad)


def solution(mesh):
    placed = (
        P("dp", "vocab"),
        P("dp", "vocab"),
        P(None, ("dp", "vocab")),
        P(("dp", "vocab")),
        P("dp", None),
        P("dp", None),
        P("dp"),
    )
    return jax.shard_map(
        shards,
        mesh=mesh,
        in_specs=placed,
        out_specs=(P(), P("dp", "vocab"), P("dp", "vocab")),
        check_vma=False,
    )
```

time: 349 us -> 199 us (0.57)
  Pallas kernels: 0 us -> 143 us
  waiting for transfers between devices: 103 us -> 0 us
  blocking collectives: 90.4 us -> 0 us
  matrix products: 69.3 us -> 0 us
  other arithmetic: 26.9 us -> 2.59 us
  between operations: 16.3 us -> 0.67 us
  local copies, waits for them, and re-layouts: 42.7 us -> 51.3 us
    pallas_call x0 -> x5, Pallas kernels: none -> 143 us  [the longest x1 39.8 us: scatter_all(): pl.pallas_call(functools.partial(scatter_kernel, groups, blocks, rows_q),...]
    reduce_scatter x2 -> x0, waiting for transfers between devices: 73.7 us -> none  [the longest x1 51 us: shards(): lax.psum_scatter(lax.dot_general(head_weight, combined, contract, preferr...]
    dot_general x6 -> x0, matrix products: 69.3 us -> none  [the longest x1 28.3 us: shards(): jnp.dot(passage_rows, head_weight, preferred_element_type=jnp.float32)]
    unnamed x3 -> x6, local copies, waits for them, and re-layouts: 2.1 us -> 45.4 us
    all_gather x4 -> x0, blocking collectives: 42.2 us -> none  [the longest x1 12.6 us: shards(): lax.all_gather(query_hidden, 'vocab', axis=1, tiled=True)]
    psum x1 -> x0, blocking collectives: 39.1 us -> none  [shards(): lax.psum((local_dots, jnp.sum(query_rep * query_rep, axis=1), jnp.sum(pas...]
    all_gather x2 -> x0, waiting for transfers between devices: 29 us -> none  [the longest x1 29 us: shards(): lax.all_gather(passage_cols, 'dp', axis=0, tiled=True)]
    convert_element_type x5 -> x1, other arithmetic: 19.3 us -> 0.01 us  [shards(): keep = small[:, :rows].astype(jnp.float32)]
  transfers between devices with their start and end apart: 4 -> 0, of which waited for: 3 -> 0; matrix products, arithmetic and copies ran while one was open for 7% -> 0% of each run, Pallas kernels for 0% -> 0%
where the time goes in v1:
time: 199 us; the launch traced here: 197 us
  Pallas kernels  143 us (72%)
  local copies, waits for them, and re-layouts  51.3 us (26%)
  other arithmetic  2.59 us (1%)
    unnamed x6, local copies, waits for them, and re-layouts  45.4 us
    pallas_call x1, Pallas kernels, scatter_all(): pl.pallas_call(functools.partial(scatter_kernel, groups, blocks, rows_q),...  39.8 us
    pallas_call x1, Pallas kernels, gather_all(): pl.pallas_call(functools.partial(gather_kernel, groups, blocks), out_shap...  32.1 us
    pallas_call x1, Pallas kernels, compute_forward(): pl.pallas_call(functools.partial(forward_kernel, segs, cols), grid=(tiles...  29.8 us
    pallas_call x1, Pallas kernels, compute_backward(): pl.pallas_call(functools.partial(backward_kernel, segs, queries, chunk),...  26.8 us
    pallas_call x1, Pallas kernels, total_all(): pl.pallas_call(functools.partial(total_kernel, groups, blocks), out_shape...  14.3 us

profile of v1, /device:TPU:0, one launch (start us, length us, event | category | flops | bytes accessed | tf_op | source)
XLA Modules:
  0.0 197.3 jit_solution(3362848954726338581)
XLA Ops:
  0.6 0.8 reshape.36
  1.4 0.8 reshape.37
  2.1 0.7 pad_add_fusion
  2.9 0.6 pad_bitcast_fusion.small_ref
  3.5 1.3 reshape.40.bias_ref
  4.8 1.5 pad_maximum_fusion.own_ref
  6.3 32.1 %shard_map.94 = (bf16[8,4,128,512]{3,2,1,0:T(8,128)(2,1)}, s32[4,8,128]{2,1,0:T(8,128)}) custom-call(bf16[128,512]{1,0:T(8,128)(2,1)} %pad_maximum_fusion.own_ref, s32[8,128]{1,0:T(8,128)} %pad_bitcast_fusion.small_ref), custom_call_target="tpu_custom_call" | custom-call | tf_op jit(solution)/shard_map/pallas_call | solution.py:292
  38.4 0.7 copy.21
  39.1 0.7 reshape.46.target_ref
  39.9 0.1 reshape.44
  40.0 0.1 reduce_sum.19
  40.1 0.1 reshape.43
  40.2 0.1 reduce_sum.18
  40.3 0.1 maximum_bitcast_fusion
  40.4 0.7 copy.16.count_ref
  41.0 0.9 copy.15.mask_ref
  41.9 41.3 %copy.14.w_ref = bf16[4096,4008]{1,0:T(8,128)(2,1)} copy(bf16[4096,4008]{0,1:T(8,128)(2,1)} %param.9) | data formatting | bytes 65667072 | tf_op args[2]
  83.2 29.8 %shard_map.95 = (bf16[512,4096]{1,0:T(8,128)(2,1)}, f32[16,4096]{1,0:T(8,128)}, f32[16,4096]{1,0:T(8,128)}, f32[16,16]{1,0:T(8,128)}) custom-call(bf16[8,512,512]{2,1,0:T(8,128)(2,1)} %bitcast.12, bf16[4096,4008]{1,0:T(8,128)(2,1)} %copy.14.w_ref, bf16[1,4008]{1,0:T(2,128)(2,1)} %reshape.40.bias_ref, f32[512,1]{1,0:T(8,128)} %copy.15.mask_ref, ...), custom_call_target="tpu_custom_call" | custom-call | tf_op jit(solution)/shard_map/pallas_call | solution.py:141
  112.9 14.3 %shard_map.96.gram_ref = f32[16,16]{1,0:T(8,128)} custom-call(f32[16,16]{1,0:T(8,128)} %get-tuple-element.15.part_ref), custom_call_target="tpu_custom_call" | custom-call | tf_op jit(solution)/shard_map/pallas_call | solution.py:348
  127.2 26.8 %shard_map.97 = (bf16[8,512,512]{2,1,0:T(8,128)(2,1)}, f32[1,1]{1,0:T(1,128)}) custom-call(f32[16,16]{1,0:T(8,128)} %shard_map.96.gram_ref, s32[8,1]{1,0:T(8,128)} %reshape.46.target_ref, f32[16,4096]{1,0:T(8,128)} %get-tuple-element.16.rep_ref, f32[16,4096]{1,0:T(8,128)} %get-tuple-element.17.inv_ref, bf16[512,4096]{1,0:T(8,128)(2,1)} %get-tuple-element.18.sig_ref, ...), custom_call_target="tpu_custom_call" | custom-call | tf_op jit(solution)/shard_map/pallas_call | solution.py:178
  154.0 2.2 %copy-done = bf16[8,512,512]{2,1,0:T(8,128)(2,1)S(1)} copy-done((bf16[8,512,512]{2,1,0:T(8,128)(2,1)S(1)}, bf16[8,512,512]{2,1,0:T(8,128)(2,1)}, u32[]{:S(2)}) %copy-start) | copy-done | bytes 4194328
  156.2 39.8 %shard_map.98 = (bf16[32,512]{1,0:T(8,128)(2,1)S(1)}, bf16[96,512]{1,0:T(8,128)(2,1)S(1)}) custom-call(bf16[8,512,512]{2,1,0:T(8,128)(2,1)S(1)} %copy-done), custom_call_target="tpu_custom_call" | custom-call | tf_op jit(solution)/shard_map/pallas_call | solution.py:434
  196.0 0.6 copy.24
  196.6 0.6 copy.25
  (4 shorter events, 0.1 us)
Async XLA Ops:
  154.0 2.2 %copy-start = (bf16[8,512,512]{2,1,0:T(8,128)(2,1)S(1)}, bf16[8,512,512]{2,1,0:T(8,128)(2,1)}, u32[]{:S(2)}) copy-start(bf16[8,512,512]{2,1,0:T(8,128)(2,1)} %get-tuple-element.20.a_ref) | copy-start | bytes 12582916
